TPU v7x, 256 devices: a whole 4x4x8 slice. The times are simulated.
256 devices in a mesh: front: 4 (over y), pivot: 8 (over x, core), rows: 8 (over z).
Axes of the slice: x: 4, y: 4, z: 8, core: 2. Of those that a mesh axis runs over, the one named last changes fastest.
Arguments:
- factor: float32 [4, 8, 1024, 8192], P('front', 'pivot', 'rows'), may hold values from -0.0625 to 0.0625
- inv_diag: float32 [4, 8, 1024, 1024], P('front', 'pivot', 'rows'), may hold values from -0.1875 to 0.1875
- boundary: float32 [4, 8192, 8192], P('front', ('pivot', 'rows')), may hold values from -0.0625 to 0.0625
- rhs: float32 [4, 240, 8192], P('front', None, ('pivot', 'rows')), may hold values from -6 to 6
- boundary_rhs: float32 [4, 240, 8192], P('front', None, ('pivot', 'rows')), may hold values from -6 to 6
- owner: int32 [4, 8192, 1], P('front', ('pivot', 'rows')), may hold values from 0 to 63; in each aligned block of 128 rows (0 to 127, 128 to 255, ..., all dimensions but the last counted through in order) at most 4 rows name the same one
- slot: int32 [4, 8192], P('front', ('pivot', 'rows')), may hold values from 0 to 255
- parent_in: float32 [240, 16384], P(None, ('pivot', 'rows')), may hold values from -6 to 6
Outputs:
- solution: float32 [4, 240, 8192], P('front', None, ('pivot', 'rows'))
- parent_rhs: float32 [240, 16384], P(None, ('pivot', 'rows'))
Inputs may be any that keep to these rules, and one draw needn't show every extreme that they name: Within the 128 boundary rows of one device no owner is named more than 4 times, and in every draw some device's rows name some owner exactly 4 times.
All inputs are finite; a program needn't handle non-finite values.
Results may differ from a plain program's by a relative error of at most 0.0001.
Values sent between devices are 32-bit elements; how exact they have to be, the bound alone decides.
A program may use at most 64 MiB of HBM per device.

v0:
```python
import jax
import jax.numpy as jnp
from jax import lax
from jax.sharding import PartitionSpec as P

highest = lax.Precision.HIGHEST


def shards(factor, inv_diag, boundary, rhs, boundary_rhs, owner, slot, parent_in):
    factor_rows = factor[0, 0]
    inv_rows = inv_diag[0, 0]
    bound_rows = boundary[0]
    local_rhs = rhs[0]
    local_brhs = boundary_rhs[0]
    block_count = lax.axis_size("pivot")
    row_count = lax.axis_size("rows")
    block_span = inv_rows.shape[1]
    slice_rows = factor_rows.shape[0]
    sources = local_rhs.shape[0]
    own_block = lax.axis_index("pivot")
    own_row = lax.axis_index("rows")
    contract = (((1,), (1,)), ((), ()))

    def solve_section(section_idx, carry):
        running, boundary_sum, own_solved = carry
        residual = local_rhs - running
        partial_value = jnp.dot(
            residual, inv_rows, precision=highest, preferred_element_type=jnp.float32
        )
        masked = jnp.where(own_block == section_idx, partial_value, 0.0)
        solved = lax.psum(masked, ("pivot", "rows"))
        pivot_tile = lax.dynamic_slice_in_dim(factor_rows, section_idx * block_span, block_span, 1)
        update_term = lax.dot_general(
            solved, pivot_tile, contract, precision=highest, preferred_element_type=jnp.float32
        )
        running = running + jnp.where(section_idx < own_block, update_term, 0.0)
        bound_tile = lax.dynamic_slice_in_dim(bound_rows, section_idx * block_span, block_span, 1)
        boundary_sum = boundary_sum + lax.dot_general(
            solved, bound_tile, contract, precision=highest, preferred_element_type=jnp.float32
        )
        own_piece = lax.dynamic_slice_in_dim(solved, own_row * slice_rows, slice_rows, 1)
        own_solved = jnp.where(own_block == section_idx, own_piece, own_solved)
        return (running, boundary_sum, own_solved)

    start = (
        jnp.zeros((sources, slice_rows), jnp.float32),
        jnp.zeros((sources, bound_rows.shape[0]), jnp.float32),
        jnp.zeros((sources, slice_rows), jnp.float32),
    )
    running, boundary_sum, own_solved = lax.fori_loop(0, block_count, solve_section, start)
    update = local_brhs - boundary_sum
    out_rows = update.T
    owners = owner[0, :, 0]
    slot_ids = slot[0]
    owner_count = block_count * row_count
    capacity = max(2, 2 * out_rows.shape[0] // owner_count)
    onehot = (owners[:, None] == jnp.arange(owner_count, dtype=jnp.int32)[None, :]).astype(
        jnp.int32
    )
    before = jnp.cumsum(onehot, axis=0) - onehot
    position = jnp.sum(before * onehot, axis=1)
    dest_slot = owners * capacity + position
    select = dest_slot[None, :] == jnp.arange(owner_count * capacity, dtype=jnp.int32)[:, None]
    send_rows = jnp.dot(
        select.astype(jnp.float32), out_rows, precision=highest, preferred_element_type=jnp.float32
    )
    send_slot = jnp.max(jnp.where(select, slot_ids[None, :], -1), axis=1)
    got_rows, got_slots = (
        lax.all_to_all(
            send_rows.reshape(owner_count, capacity, sources),
            ("pivot", "rows"),
            split_axis=0,
            concat_axis=0,
            tiled=True,
        ),
        lax.all_to_all(
            send_slot.reshape(owner_count, capacity),
            ("pivot", "rows"),
            split_axis=0,
            concat_axis=0,
            tiled=True,
        ),
    )
    got_rows = got_rows.reshape(owner_count * capacity, sources)
    got_slots = got_slots.reshape(owner_count * capacity)
    parent_rows = parent_in.shape[1]
    slot_hits = (got_slots[:, None] == jnp.arange(parent_rows, dtype=jnp.int32)[None, :]).astype(
        jnp.float32
    )
    local_part = jnp.einsum(
        "ks,ko->so", got_rows, slot_hits, precision=highest, preferred_element_type=jnp.float32
    )
    sibling_total = lax.psum(local_part, "front")
    parent = parent_in + sibling_total
    return (own_solved[None], parent)


def solution(mesh):
    placed = (
        P("front", "pivot", "rows", None),
        P("front", "pivot", "rows", None),
        P("front", ("pivot", "rows"), None),
        P("front", None, ("pivot", "rows")),
        P("front", None, ("pivot", "rows")),
        P("front", ("pivot", "rows"), None),
        P("front", ("pivot", "rows")),
        P(None, ("pivot", "rows")),
    )
    return jax.shard_map(
        shards,
        mesh=mesh,
        in_specs=placed,
        out_specs=(P("front", None, ("pivot", "rows")), P(None, ("pivot", "rows"))),
        check_vma=False,
    )
```

profile of v0, /device:TPU:2, one launch (start us, length us, event | category | flops | bytes accessed | tf_op | source)
XLA Modules:
  0.0 1667.7 jit_solution(10472206007967670768)
XLA Ops:
  11.9 12.0 all-to-all-start.1
  24.0 1568.2 %while.20 = (s32[]{:T(128)}, f32[240,128]{1,0:T(8,128)S(1)}, f32[240,128]{1,0:T(8,128)S(1)}, f32[240,128]{1,0:T(8,128)S(1)}, s32[]{:T(128)}, /*index=5*/f32[240,...) while((s32[]{:T(128)}, f32[240,128]{1,0:T(8,128)S(1)}, ...), condition=%wide.region_2.3_spmd.clone, body=%wide.region_0.2_spmd.clone.sunk | while | flops 1133230080 | bytes 11526409 | solution.py:50
  24.1 3.1 convolution_select_fusion.3
  27.2 189.0 %all-reduce.5.cloned.1.call-done = f32[240,1024]{1,0:T(8,128)} async-done(((f32[240,1024]{1,0:T(8,128)}), f32[240,1024]{1,0:T(8,128)}) %all-reduce.5.cloned.1.call-update) | async-done | bytes 983056 | tf_op jit(solution)/shard_map/while/body/eval_jaxpr/psum | solution.py:31
  216.2 2.3 convolution_add_fusion.2
  221.9 3.0 convolution_select_fusion.3
  224.9 187.0 %all-reduce.5.cloned.1.call-done = f32[240,1024]{1,0:T(8,128)} async-done(((f32[240,1024]{1,0:T(8,128)}), f32[240,1024]{1,0:T(8,128)}) %all-reduce.5.cloned.1.call-update) | async-done | bytes 983056 | tf_op jit(solution)/shard_map/while/body/eval_jaxpr/psum | solution.py:31
  411.9 2.3 convolution_add_fusion.2
  414.3 2.3 fusion.32
  417.6 3.0 convolution_select_fusion.3
  420.7 187.0 %all-reduce.5.cloned.1.call-done = f32[240,1024]{1,0:T(8,128)} async-done(((f32[240,1024]{1,0:T(8,128)}), f32[240,1024]{1,0:T(8,128)}) %all-reduce.5.cloned.1.call-update) | async-done | bytes 983056 | tf_op jit(solution)/shard_map/while/body/eval_jaxpr/psum | solution.py:31
  607.7 2.3 convolution_add_fusion.2
  610.0 2.3 fusion.32
  613.3 3.0 convolution_select_fusion.3
  616.4 186.7 %all-reduce.5.cloned.1.call-done = f32[240,1024]{1,0:T(8,128)} async-done(((f32[240,1024]{1,0:T(8,128)}), f32[240,1024]{1,0:T(8,128)}) %all-reduce.5.cloned.1.call-update) | async-done | bytes 983056 | tf_op jit(solution)/shard_map/while/body/eval_jaxpr/psum | solution.py:31
  803.1 2.3 convolution_add_fusion.2
  808.7 3.0 convolution_select_fusion.3
  811.8 186.7 %all-reduce.5.cloned.1.call-done = f32[240,1024]{1,0:T(8,128)} async-done(((f32[240,1024]{1,0:T(8,128)}), f32[240,1024]{1,0:T(8,128)}) %all-reduce.5.cloned.1.call-update) | async-done | bytes 983056 | tf_op jit(solution)/shard_map/while/body/eval_jaxpr/psum | solution.py:31
  998.5 2.3 convolution_add_fusion.2
  1004.2 3.0 convolution_select_fusion.3
  1007.2 187.4 %all-reduce.5.cloned.1.call-done = f32[240,1024]{1,0:T(8,128)} async-done(((f32[240,1024]{1,0:T(8,128)}), f32[240,1024]{1,0:T(8,128)}) %all-reduce.5.cloned.1.call-update) | async-done | bytes 983056 | tf_op jit(solution)/shard_map/while/body/eval_jaxpr/psum | solution.py:31
  1194.6 2.3 convolution_add_fusion.2
  1200.3 3.0 convolution_select_fusion.3
  1203.4 187.4 %all-reduce.5.cloned.1.call-done = f32[240,1024]{1,0:T(8,128)} async-done(((f32[240,1024]{1,0:T(8,128)}), f32[240,1024]{1,0:T(8,128)}) %all-reduce.5.cloned.1.call-update) | async-done | bytes 983056 | tf_op jit(solution)/shard_map/while/body/eval_jaxpr/psum | solution.py:31
  1390.8 2.3 convolution_add_fusion.2
  1393.2 2.3 fusion.32
  1396.5 3.0 convolution_select_fusion.3
  1399.6 187.0 %all-reduce.5.cloned.1.call-done = f32[240,1024]{1,0:T(8,128)} async-done(((f32[240,1024]{1,0:T(8,128)}), f32[240,1024]{1,0:T(8,128)}) %all-reduce.5.cloned.1.call-update) | async-done | bytes 983056 | tf_op jit(solution)/shard_map/while/body/eval_jaxpr/psum | solution.py:31
  1586.6 2.3 convolution_add_fusion.2
  1593.3 8.3 all-to-all-start
  1603.0 11.3 all-to-all-done
  1615.6 43.0 %all-reduce.3.cloned.1.call-done = f32[240,256]{1,0:T(8,128)} async-done(((f32[240,256]{1,0:T(8,128)}), f32[240,256]{1,0:T(8,128)}) %all-reduce.3.cloned.1.call-update) | async-done | bytes 245776 | tf_op jit(solution)/shard_map/psum | solution.py:93
  (55 shorter events, 28.9 us)
Async XLA Ops:
  11.9 1581.4 %all-to-all-start.1 = ((s32[64,1,4]{2,1,0:T(1,128)}), s32[64,1,4]{2,1,0:T(1,128)S(1)}, u32[]{:S(2)}, u32[]{:S(2)}) async-start(s32[64,1,4]{2,1,0:T(1,128)} %bitcast.8), calls=%async_computation.1 | async-start | bytes 65536 | tf_op jit(solution)/shard_map/all_to_all | solution.py:76
  24.0 1568.2 %copy-start.2 = (f32[1,240,128]{2,1,0:T(8,128)S(1)}, f32[1,240,128]{2,1,0:T(8,128)}, u32[]{:S(2)}) copy-start(f32[1,240,128]{2,1,0:T(8,128)} %param.14) | copy-start | bytes 368644
  24.0 1634.6 %copy-start.1 = (f32[240,256]{1,0:T(8,128)S(1)}, f32[240,256]{1,0:T(8,128)}, u32[]{:S(2)}) copy-start(f32[240,256]{1,0:T(8,128)} %param.17) | copy-start | bytes 737284
  24.0 192.2 %all-reduce.5.cloned.1.call-start = ((), (), s32[]{:S(2)}) async-start(), calls=%async_computation.3 | async-start | bytes 1966080 | tf_op jit(solution)/shard_map/while/body/eval_jaxpr/psum | solution.py:31
  221.8 190.1 %all-reduce.5.cloned.1.call-start = ((), (), s32[]{:S(2)}) async-start(), calls=%async_computation.3 | async-start | bytes 1966080 | tf_op jit(solution)/shard_map/while/body/eval_jaxpr/psum | solution.py:31
  417.6 190.1 %all-reduce.5.cloned.1.call-start = ((), (), s32[]{:S(2)}) async-start(), calls=%async_computation.3 | async-start | bytes 1966080 | tf_op jit(solution)/shard_map/while/body/eval_jaxpr/psum | solution.py:31
  613.3 189.8 %all-reduce.5.cloned.1.call-start = ((), (), s32[]{:S(2)}) async-start(), calls=%async_computation.3 | async-start | bytes 1966080 | tf_op jit(solution)/shard_map/while/body/eval_jaxpr/psum | solution.py:31
  808.7 189.8 %all-reduce.5.cloned.1.call-start = ((), (), s32[]{:S(2)}) async-start(), calls=%async_computation.3 | async-start | bytes 1966080 | tf_op jit(solution)/shard_map/while/body/eval_jaxpr/psum | solution.py:31
  1004.1 190.5 %all-reduce.5.cloned.1.call-start = ((), (), s32[]{:S(2)}) async-start(), calls=%async_computation.3 | async-start | bytes 1966080 | tf_op jit(solution)/shard_map/while/body/eval_jaxpr/psum | solution.py:31
  1200.3 190.6 %all-reduce.5.cloned.1.call-start = ((), (), s32[]{:S(2)}) async-start(), calls=%async_computation.3 | async-start | bytes 1966080 | tf_op jit(solution)/shard_map/while/body/eval_jaxpr/psum | solution.py:31
  1396.4 190.2 %all-reduce.5.cloned.1.call-start = ((), (), s32[]{:S(2)}) async-start(), calls=%async_computation.3 | async-start | bytes 1966080 | tf_op jit(solution)/shard_map/while/body/eval_jaxpr/psum | solution.py:31
  1592.2 68.1 %copy-start = (f32[240,128]{1,0:T(8,128)}, f32[240,128]{1,0:T(8,128)S(1)}, u32[]{:S(2)}) copy-start(f32[240,128]{1,0:T(8,128)S(1)} %get-tuple-element.239) | copy-start | bytes 368644
  1593.3 21.0 %all-to-all-start = ((f32[64,4,240]{2,1,0:T(4,128)}), f32[64,4,240]{2,1,0:T(4,128)S(1)}, u32[]{:S(2)}, u32[]{:S(2)}) async-start(f32[64,4,240]{2,1,0:T(4,128)} %reshape.25), calls=%async_computation | async-start | bytes 524288 | tf_op jit(solution)/shard_map/all_to_all | solution.py:69
  1601.6 56.9 %all-reduce.3.cloned.1.call-start = ((), (), s32[]{:S(2)}) async-start(), calls=%async_computation.2 | async-start | bytes 491520 | tf_op jit(solution)/shard_map/psum | solution.py:93
Sparse Core Ops, SparseCore 0:
  28.2 187.9 all-reduce.4
  226.0 185.8 all-reduce.4
  421.7 185.8 all-reduce.4
  617.2 185.8 all-reduce.4
  812.6 185.8 all-reduce.4
  1008.0 186.6 all-reduce.4
  1204.5 186.3 all-reduce.4
  1400.6 185.9 all-reduce.4
Sparse Core Ops, SparseCore 1:
  1615.7 42.8 all-reduce.2
where the time goes:
time: 1670 us
  waiting for transfers between devices  1550 us (93%)
  matrix products  62.8 us (4%)
  starting transfers between devices  20.7 us (1%)
    psum x8, waiting for transfers between devices, solve_section(): solved = lax.psum(masked, ('pivot', 'rows'))  1500 us
    psum x1, waiting for transfers between devices, shards(): sibling_total = lax.psum(local_part, 'front')  43 us
  transfers between devices with their start and end apart: 11, of which 10 were waited for; matrix products, arithmetic and copies ran while one was open for 4% of the time, Pallas kernels for 0%

commit v1 on v0

--- a/solution.py
+++ b/solution.py
@@ -28,7 +28,7 @@
             residual, inv_rows, precision=highest, preferred_element_type=jnp.float32
         )
         masked = jnp.where(own_block == section_idx, partial_value, 0.0)
-        solved = lax.psum(masked, ("pivot", "rows"))
+        solved = lax.psum(lax.psum(masked, "pivot"), "rows")
         pivot_tile = lax.dynamic_slice_in_dim(factor_rows, section_idx * block_span, block_span, 1)
         update_term = lax.dot_general(
             solved, pivot_tile, contract, precision=highest, preferred_element_type=jnp.float32

time: 1670 us -> 1320 us (0.79)
  waiting for transfers between devices: 1550 us -> 1200 us
    psum x8 -> x16, waiting for transfers between devices: 1500 us -> 1150 us  [solve_section(): solved = lax.psum(lax.psum(masked, 'pivot'), 'rows')]
  transfers between devices with their start and end apart: 11 -> 19, of which waited for: 10 -> 18; matrix products, arithmetic and copies ran while one was open for 4% -> 5% of each run, Pallas kernels for 0% -> 0%
where the time goes in v1:
time: 1320 us
  waiting for transfers between devices  1200 us (91%)
  matrix products  62.8 us (5%)
  starting transfers between devices  20.4 us (2%)
  between operations  15.3 us (1%)
    psum x16, waiting for transfers between devices, solve_section(): solved = lax.psum(lax.psum(masked, 'pivot'), 'rows')  1150 us
    psum x1, waiting for transfers between devices, shards(): sibling_total = lax.psum(local_part, 'front')  43 us
  transfers between devices with their start and end apart: 19, of which 18 were waited for; matrix products, arithmetic and copies ran while one was open for 5% of the time, Pallas kernels for 0%

profile of v1, /device:TPU:2, one launch (start us, length us, event | category | flops | bytes accessed | tf_op | source)
XLA Modules:
  0.0 1317.1 jit_solution(11716667460887189944)
XLA Ops:
  11.9 12.0 all-to-all-start.1
  24.0 1218.5 %while.20 = (s32[]{:T(128)}, f32[240,128]{1,0:T(8,128)S(1)}, f32[240,128]{1,0:T(8,128)S(1)}, f32[240,128]{1,0:T(8,128)S(1)}, s32[]{:T(128)}, /*index=5*/f32[240,...) while((s32[]{:T(128)}, f32[240,128]{1,0:T(8,128)S(1)}, ...), condition=%wide.region_3.4_spmd.clone, body=%wide.region_0.3_spmd.clone.sunk | while | flops 1133475840 | bytes 17424688 | solution.py:50
  24.1 3.1 convolution_select_fusion.3
  27.2 66.6 %all-reduce.6.cloned.1.call-done = f32[240,1024]{1,0:T(8,128)} async-done(((f32[240,1024]{1,0:T(8,128)}), f32[240,1024]{1,0:T(8,128)}) %all-reduce.6.cloned.1.call-update) | async-done | bytes 983056 | tf_op jit(solution)/shard_map/while/body/eval_jaxpr/psum | solution.py:31
  93.9 79.5 %all-reduce.8.cloned.1.call-done = f32[240,1024]{1,0:T(8,128)} async-done(((f32[240,1024]{1,0:T(8,128)}), f32[240,1024]{1,0:T(8,128)}) %all-reduce.8.cloned.1.call-update) | async-done | bytes 983056 | tf_op jit(solution)/shard_map/while/body/eval_jaxpr/psum | solution.py:31
  179.1 3.0 convolution_select_fusion.3
  182.2 63.7 %all-reduce.6.cloned.1.call-done = f32[240,1024]{1,0:T(8,128)} async-done(((f32[240,1024]{1,0:T(8,128)}), f32[240,1024]{1,0:T(8,128)}) %all-reduce.6.cloned.1.call-update) | async-done | bytes 983056 | tf_op jit(solution)/shard_map/while/body/eval_jaxpr/psum | solution.py:31
  246.0 79.4 %all-reduce.8.cloned.1.call-done = f32[240,1024]{1,0:T(8,128)} async-done(((f32[240,1024]{1,0:T(8,128)}), f32[240,1024]{1,0:T(8,128)}) %all-reduce.8.cloned.1.call-update) | async-done | bytes 983056 | tf_op jit(solution)/shard_map/while/body/eval_jaxpr/psum | solution.py:31
  325.3 2.3 convolution_add_fusion.2
  331.0 3.0 convolution_select_fusion.3
  334.1 63.7 %all-reduce.6.cloned.1.call-done = f32[240,1024]{1,0:T(8,128)} async-done(((f32[240,1024]{1,0:T(8,128)}), f32[240,1024]{1,0:T(8,128)}) %all-reduce.6.cloned.1.call-update) | async-done | bytes 983056 | tf_op jit(solution)/shard_map/while/body/eval_jaxpr/psum | solution.py:31
  397.8 79.4 %all-reduce.8.cloned.1.call-done = f32[240,1024]{1,0:T(8,128)} async-done(((f32[240,1024]{1,0:T(8,128)}), f32[240,1024]{1,0:T(8,128)}) %all-reduce.8.cloned.1.call-update) | async-done | bytes 983056 | tf_op jit(solution)/shard_map/while/body/eval_jaxpr/psum | solution.py:31
  482.9 3.0 convolution_select_fusion.3
  486.0 63.7 %all-reduce.6.cloned.1.call-done = f32[240,1024]{1,0:T(8,128)} async-done(((f32[240,1024]{1,0:T(8,128)}), f32[240,1024]{1,0:T(8,128)}) %all-reduce.6.cloned.1.call-update) | async-done | bytes 983056 | tf_op jit(solution)/shard_map/while/body/eval_jaxpr/psum | solution.py:31
  549.7 79.5 %all-reduce.8.cloned.1.call-done = f32[240,1024]{1,0:T(8,128)} async-done(((f32[240,1024]{1,0:T(8,128)}), f32[240,1024]{1,0:T(8,128)}) %all-reduce.8.cloned.1.call-update) | async-done | bytes 983056 | tf_op jit(solution)/shard_map/while/body/eval_jaxpr/psum | solution.py:31
  634.9 3.0 convolution_select_fusion.3
  638.0 63.7 %all-reduce.6.cloned.1.call-done = f32[240,1024]{1,0:T(8,128)} async-done(((f32[240,1024]{1,0:T(8,128)}), f32[240,1024]{1,0:T(8,128)}) %all-reduce.6.cloned.1.call-update) | async-done | bytes 983056 | tf_op jit(solution)/shard_map/while/body/eval_jaxpr/psum | solution.py:31
  701.8 79.3 %all-reduce.8.cloned.1.call-done = f32[240,1024]{1,0:T(8,128)} async-done(((f32[240,1024]{1,0:T(8,128)}), f32[240,1024]{1,0:T(8,128)}) %all-reduce.8.cloned.1.call-update) | async-done | bytes 983056 | tf_op jit(solution)/shard_map/while/body/eval_jaxpr/psum | solution.py:31
  786.8 3.0 convolution_select_fusion.3
  789.9 63.7 %all-reduce.6.cloned.1.call-done = f32[240,1024]{1,0:T(8,128)} async-done(((f32[240,1024]{1,0:T(8,128)}), f32[240,1024]{1,0:T(8,128)}) %all-reduce.6.cloned.1.call-update) | async-done | bytes 983056 | tf_op jit(solution)/shard_map/while/body/eval_jaxpr/psum | solution.py:31
  853.7 79.4 %all-reduce.8.cloned.1.call-done = f32[240,1024]{1,0:T(8,128)} async-done(((f32[240,1024]{1,0:T(8,128)}), f32[240,1024]{1,0:T(8,128)}) %all-reduce.8.cloned.1.call-update) | async-done | bytes 983056 | tf_op jit(solution)/shard_map/while/body/eval_jaxpr/psum | solution.py:31
  933.0 2.3 convolution_add_fusion.2
  938.7 3.0 convolution_select_fusion.3
  941.8 63.7 %all-reduce.6.cloned.1.call-done = f32[240,1024]{1,0:T(8,128)} async-done(((f32[240,1024]{1,0:T(8,128)}), f32[240,1024]{1,0:T(8,128)}) %all-reduce.6.cloned.1.call-update) | async-done | bytes 983056 | tf_op jit(solution)/shard_map/while/body/eval_jaxpr/psum | solution.py:31
  1005.6 79.4 %all-reduce.8.cloned.1.call-done = f32[240,1024]{1,0:T(8,128)} async-done(((f32[240,1024]{1,0:T(8,128)}), f32[240,1024]{1,0:T(8,128)}) %all-reduce.8.cloned.1.call-update) | async-done | bytes 983056 | tf_op jit(solution)/shard_map/while/body/eval_jaxpr/psum | solution.py:31
  1090.6 3.0 convolution_select_fusion.3
  1093.7 63.7 %all-reduce.6.cloned.1.call-done = f32[240,1024]{1,0:T(8,128)} async-done(((f32[240,1024]{1,0:T(8,128)}), f32[240,1024]{1,0:T(8,128)}) %all-reduce.6.cloned.1.call-update) | async-done | bytes 983056 | tf_op jit(solution)/shard_map/while/body/eval_jaxpr/psum | solution.py:31
  1157.5 79.4 %all-reduce.8.cloned.1.call-done = f32[240,1024]{1,0:T(8,128)} async-done(((f32[240,1024]{1,0:T(8,128)}), f32[240,1024]{1,0:T(8,128)}) %all-reduce.8.cloned.1.call-update) | async-done | bytes 983056 | tf_op jit(solution)/shard_map/while/body/eval_jaxpr/psum | solution.py:31
  1236.9 2.3 convolution_add_fusion.2
  1243.6 7.7 all-to-all-start
  1252.7 11.3 all-to-all-done
  1265.3 43.0 %all-reduce.4.cloned.1.call-done = f32[240,256]{1,0:T(8,128)} async-done(((f32[240,256]{1,0:T(8,128)}), f32[240,256]{1,0:T(8,128)}) %all-reduce.4.cloned.1.call-update) | async-done | bytes 245776 | tf_op jit(solution)/shard_map/psum | solution.py:93
  (79 shorter events, 47.9 us)
Async XLA Ops:
  11.9 1231.7 %all-to-all-start.1 = ((s32[64,1,4]{2,1,0:T(1,128)}), s32[64,1,4]{2,1,0:T(1,128)S(1)}, u32[]{:S(2)}, u32[]{:S(2)}) async-start(s32[64,1,4]{2,1,0:T(1,128)} %bitcast.8), calls=%async_computation.1 | async-start | bytes 65536 | tf_op jit(solution)/shard_map/all_to_all | solution.py:76
  24.0 1218.6 %copy-start.2 = (f32[1,240,128]{2,1,0:T(8,128)S(1)}, f32[1,240,128]{2,1,0:T(8,128)}, u32[]{:S(2)}) copy-start(f32[1,240,128]{2,1,0:T(8,128)} %param.14) | copy-start | bytes 368644
  24.0 1284.3 %copy-start.1 = (f32[240,256]{1,0:T(8,128)S(1)}, f32[240,256]{1,0:T(8,128)}, u32[]{:S(2)}) copy-start(f32[240,256]{1,0:T(8,128)} %param.17) | copy-start | bytes 737284
  24.0 69.9 %all-reduce.6.cloned.1.call-start = ((), (), s32[]{:S(2)}) async-start(), calls=%async_computation.3 | async-start | bytes 1966080 | tf_op jit(solution)/shard_map/while/body/eval_jaxpr/psum | solution.py:31
  27.2 146.2 %all-reduce.8.cloned.1.call-start = ((), (), s32[]{:S(2)}) async-start(), calls=%async_computation.4 | async-start | bytes 1966080 | tf_op jit(solution)/shard_map/while/body/eval_jaxpr/psum | solution.py:31
  179.0 66.9 %all-reduce.6.cloned.1.call-start = ((), (), s32[]{:S(2)}) async-start(), calls=%async_computation.3 | async-start | bytes 1966080 | tf_op jit(solution)/shard_map/while/body/eval_jaxpr/psum | solution.py:31
  182.1 143.2 %all-reduce.8.cloned.1.call-start = ((), (), s32[]{:S(2)}) async-start(), calls=%async_computation.4 | async-start | bytes 1966080 | tf_op jit(solution)/shard_map/while/body/eval_jaxpr/psum | solution.py:31
  330.9 66.9 %all-reduce.6.cloned.1.call-start = ((), (), s32[]{:S(2)}) async-start(), calls=%async_computation.3 | async-start | bytes 1966080 | tf_op jit(solution)/shard_map/while/body/eval_jaxpr/psum | solution.py:31
  334.0 143.2 %all-reduce.8.cloned.1.call-start = ((), (), s32[]{:S(2)}) async-start(), calls=%async_computation.4 | async-start | bytes 1966080 | tf_op jit(solution)/shard_map/while/body/eval_jaxpr/psum | solution.py:31
  482.8 66.9 %all-reduce.6.cloned.1.call-start = ((), (), s32[]{:S(2)}) async-start(), calls=%async_computation.3 | async-start | bytes 1966080 | tf_op jit(solution)/shard_map/while/body/eval_jaxpr/psum | solution.py:31
  485.9 143.3 %all-reduce.8.cloned.1.call-start = ((), (), s32[]{:S(2)}) async-start(), calls=%async_computation.4 | async-start | bytes 1966080 | tf_op jit(solution)/shard_map/while/body/eval_jaxpr/psum | solution.py:31
  634.9 66.9 %all-reduce.6.cloned.1.call-start = ((), (), s32[]{:S(2)}) async-start(), calls=%async_computation.3 | async-start | bytes 1966080 | tf_op jit(solution)/shard_map/while/body/eval_jaxpr/psum | solution.py:31
  638.0 143.2 %all-reduce.8.cloned.1.call-start = ((), (), s32[]{:S(2)}) async-start(), calls=%async_computation.4 | async-start | bytes 1966080 | tf_op jit(solution)/shard_map/while/body/eval_jaxpr/psum | solution.py:31
  786.7 66.9 %all-reduce.6.cloned.1.call-start = ((), (), s32[]{:S(2)}) async-start(), calls=%async_computation.3 | async-start | bytes 1966080 | tf_op jit(solution)/shard_map/while/body/eval_jaxpr/psum | solution.py:31
  789.9 143.2 %all-reduce.8.cloned.1.call-start = ((), (), s32[]{:S(2)}) async-start(), calls=%async_computation.4 | async-start | bytes 1966080 | tf_op jit(solution)/shard_map/while/body/eval_jaxpr/psum | solution.py:31
  938.6 66.9 %all-reduce.6.cloned.1.call-start = ((), (), s32[]{:S(2)}) async-start(), calls=%async_computation.3 | async-start | bytes 1966080 | tf_op jit(solution)/shard_map/while/body/eval_jaxpr/psum | solution.py:31
  941.8 143.2 %all-reduce.8.cloned.1.call-start = ((), (), s32[]{:S(2)}) async-start(), calls=%async_computation.4 | async-start | bytes 1966080 | tf_op jit(solution)/shard_map/while/body/eval_jaxpr/psum | solution.py:31
  1090.5 66.9 %all-reduce.6.cloned.1.call-start = ((), (), s32[]{:S(2)}) async-start(), calls=%async_computation.3 | async-start | bytes 1966080 | tf_op jit(solution)/shard_map/while/body/eval_jaxpr/psum | solution.py:31
  1093.7 143.3 %all-reduce.8.cloned.1.call-start = ((), (), s32[]{:S(2)}) async-start(), calls=%async_computation.4 | async-start | bytes 1966080 | tf_op jit(solution)/shard_map/while/body/eval_jaxpr/psum | solution.py:31
  1242.5 67.5 %copy-start = (f32[240,128]{1,0:T(8,128)}, f32[240,128]{1,0:T(8,128)S(1)}, u32[]{:S(2)}) copy-start(f32[240,128]{1,0:T(8,128)S(1)} %get-tuple-element.239) | copy-start | bytes 368644
  1243.6 20.4 %all-to-all-start = ((f32[64,4,240]{2,1,0:T(4,128)}), f32[64,4,240]{2,1,0:T(4,128)S(1)}, u32[]{:S(2)}, u32[]{:S(2)}) async-start(f32[64,4,240]{2,1,0:T(4,128)} %reshape.25), calls=%async_computation | async-start | bytes 524288 | tf_op jit(solution)/shard_map/all_to_all | solution.py:69
  1251.3 56.9 %all-reduce.4.cloned.1.call-start = ((), (), s32[]{:S(2)}) async-start(), calls=%async_computation.2 | async-start | bytes 491520 | tf_op jit(solution)/shard_map/psum | solution.py:93
Sparse Core Ops, SparseCore 0:
  27.3 66.5 all-reduce.5
  96.2 77.1 all-reduce.7
  182.2 63.6 all-reduce.5
  248.1 77.1 all-reduce.7
  334.1 63.6 all-reduce.5
  400.0 77.1 all-reduce.7
  486.0 63.6 all-reduce.5
  552.1 77.1 all-reduce.7
  638.1 63.6 all-reduce.5
  704.0 77.1 all-reduce.7
  790.0 63.6 all-reduce.5
  855.9 77.1 all-reduce.7
  941.9 63.6 all-reduce.5
  1007.8 77.1 all-reduce.7
  1093.8 63.6 all-reduce.5
  1159.7 77.2 all-reduce.7
Sparse Core Ops, SparseCore 1:
  1265.4 42.9 all-reduce.3
